TPU v7x, 32 devices: a whole 2x2x4 slice. The times are simulated.
32 devices in a mesh: wave: 8 (over z, y), lev: 4 (over x, core).
Axes of the slice: x: 2, y: 2, z: 4, core: 2. Of those that a mesh axis runs over, the one named last changes fastest.
Arguments:
- fine_state: float32 [8, 3, 2, 24, 49], P('lev', None, None, 'wave'), may hold values from -6 to 6
- fold_pairs: int32 [24], replicated, may hold values from 0 to 23, each once
- legendre: bfloat16 [24, 96, 49], P('wave', 'lev'), may hold values from -0.875 to 0.875
- gauss_weights: float32 [96], P('lev'), may hold values from 0.5 to 3
- grid_coef: float32 [8, 2560], replicated, may hold values from -4 to 4
- modes_from: float32 [8, 8], replicated
- modes_to: float32 [8, 8], replicated, as said below
- mode_rates: float32 [8], replicated, may hold values from 0.2 to 20
Outputs:
- corrected: float32 [8, 2, 2, 24, 49], P('lev', None, None, 'wave')
- fine_tend: float32 [8, 3, 2, 24, 49], P('lev', None, None, 'wave')
Inputs may be any that keep to these rules, and one draw needn't show every extreme that they name: Slot p holds zonal wavenumbers fold_pairs[p] and 47 - fold_pairs[p]; every value occurs once. modes_to is the inverse of modes_from.
All inputs are finite; a program needn't handle non-finite values.
Results may differ from a plain program's by a relative error of at most 0.02.
Values may be sent and summed in bfloat16 or wider, within the bound.
No kernel may reach another device: no remote copies, remote signals or barrier semaphores. Data moves between devices by JAX's collectives and lax.ppermute only.
A program may use at most 64 MiB of HBM per device.

v0:
```python
import math
import jax
import jax.numpy as jnp
from jax import lax
from jax.sharding import PartitionSpec as P

STEP_HALF = 0.5
quad_weights = ((5.0 / 24.0, 1.0 / 3.0, -1.0 / 24.0), (-1.0 / 24.0, 1.0 / 3.0, 5.0 / 24.0))
HIGHEST = lax.Precision.HIGHEST


def fourier_table(waves, points, amplitude):
    steps = jnp.arange(points, dtype=jnp.int32)
    turns = waves[:, :, None] * steps[None, None, :] % points
    angles = turns.astype(jnp.float32) * (2.0 * math.pi / points)
    return jnp.stack([jnp.cos(angles) * amplitude, -jnp.sin(angles) * amplitude]).astype(
        jnp.bfloat16
    )


def fine_rows(small_wave, fine_width):
    row_ids = jnp.arange(fine_width + 1, dtype=jnp.int32)[None, :]
    return row_ids < fine_width - small_wave[:, None]


def coarse_rows(small_wave, coarse):
    row_ids = jnp.arange(coarse, dtype=jnp.int32)[None, :]
    coarse_keep = row_ids < coarse - small_wave[:, None]
    degree = (small_wave[:, None] + row_ids).astype(jnp.float32)
    return (coarse_keep, degree)


def legendre_inverse(spectral, legendre_table, row_mask):
    split_spec = spectral[:, :, :, :, None, :] * row_mask[None, None, None]
    return jnp.einsum(
        "abcpmr,plr->abcpml", split_spec, legendre_table, preferred_element_type=jnp.float32
    ).astype(jnp.bfloat16)


def legendre_forward(returned, legendre_table, row_mask):
    members = jnp.einsum(
        "abcpml,plr->abcpmr", returned, legendre_table, preferred_element_type=jnp.float32
    )
    return jnp.sum(members * row_mask.astype(jnp.float32)[None, None, None], axis=4)


def grid_step(fourier, wave_table, coef, weights, factor):
    grid_field = jnp.einsum(
        "abcpmz,cpmk->abzk", fourier, wave_table, preferred_element_type=jnp.float32
    )
    product = (coef[:, None, None, :] * grid_field * grid_field).astype(jnp.bfloat16)
    returned = jnp.einsum(
        "abzk,cpmk->abcpmz", product, wave_table, preferred_element_type=jnp.float32
    )
    return (returned * (weights * factor)).astype(jnp.bfloat16)


def mix(matrix, values):
    return jnp.einsum("ql,lbcpr->qbcpr", matrix, values, precision=HIGHEST)


def per_device(
    fine_state, fold_pairs, legendre, gauss_weights, grid_coef, modes_from, modes_to, mode_rates
):
    n_wave = lax.axis_size("wave")
    wave_idx = lax.axis_index("wave")
    lev_idx = lax.axis_index("lev")
    lev_dev = fine_state.shape[0]
    pairs_dev = fine_state.shape[3]
    fine_width = fine_state.shape[4] - 1
    coarse = fine_width // 2
    longitudes = grid_coef.shape[1]
    band_size = legendre.shape[1] // n_wave
    small_wave = lax.dynamic_slice_in_dim(fold_pairs, wave_idx * pairs_dev, pairs_dev)
    first_member = fine_rows(small_wave, fine_width)
    member_mask = jnp.stack([first_member, jnp.logical_not(first_member)], 1).astype(jnp.bfloat16)
    coarse_keep, degree = coarse_rows(small_wave, coarse)
    keep_mask = coarse_keep[:, None, :].astype(jnp.bfloat16)
    keep_float = coarse_keep.astype(jnp.float32)
    fine_table = fourier_table(
        jnp.stack([fold_pairs, fine_width - 1 - fold_pairs], 1), longitudes, fine_width ** (-0.5)
    )
    coarse_table = fourier_table(fold_pairs[:, None], longitudes // 2, coarse ** (-0.5))
    coarse_leg = legendre[:, :, :coarse]
    coarse_coef = grid_coef[:, ::2]
    band_gauss = lax.dynamic_slice_in_dim(gauss_weights, wave_idx * band_size, band_size)
    local_to = lax.dynamic_slice_in_dim(modes_to, lev_idx * lev_dev, lev_dev, 1)
    local_from = lax.dynamic_slice_in_dim(modes_from, lev_idx * lev_dev, lev_dev, 1)
    mode_decay = lax.dynamic_slice_in_dim(mode_rates, lev_idx * lev_dev, lev_dev)

    def project(partial_sum):
        return mix(modes_to, partial_sum)

    def coarse_start(modes):
        gathered = lax.all_gather(modes, "lev", axis=0, tiled=True)
        levels = (mix(modes_from, gathered) * keep_float).astype(jnp.bfloat16)
        return legendre_inverse(levels, coarse_leg, keep_mask)

    def coarse_grid_step(fourier):
        return grid_step(
            fourier, coarse_table, coarse_coef, band_gauss, 2.0 * coarse / (longitudes // 2)
        )

    def coarse_finish(returned):
        partial_sum = legendre_forward(returned, coarse_leg, keep_mask)
        return lax.psum_scatter(
            project(partial_sum).astype(jnp.bfloat16), "lev", scatter_dimension=0, tiled=True
        ).astype(jnp.float32)

    def coarse_eval(modes):
        fourier = lax.all_to_all(
            coarse_start(modes), "wave", split_axis=5, concat_axis=3, tiled=True
        )
        returned = lax.all_to_all(
            coarse_grid_step(fourier), "wave", split_axis=3, concat_axis=5, tiled=True
        )
        return coarse_finish(returned)

    restricted = fine_state[..., :coarse] * keep_float
    fine_spec = lax.all_gather(fine_state.astype(jnp.bfloat16), "lev", axis=0, tiled=True)
    fine_fourier = legendre_inverse(fine_spec, legendre, member_mask)
    fine_fourier = lax.all_to_all(fine_fourier, "wave", split_axis=5, concat_axis=3, tiled=True)
    fine_back = lax.all_to_all(
        grid_step(fine_fourier, fine_table, grid_coef, band_gauss, 2.0 * fine_width / longitudes),
        "wave",
        split_axis=3,
        concat_axis=5,
        tiled=True,
    )
    fine_tend = lax.psum_scatter(
        legendre_forward(fine_back, legendre, member_mask).astype(jnp.bfloat16),
        "lev",
        scatter_dimension=0,
        tiled=True,
    ).astype(jnp.float32)
    restricted_tend = fine_tend[..., :coarse] * keep_float
    stacked = jnp.concatenate([restricted, restricted_tend], 1)
    both_modes = lax.psum_scatter(
        mix(local_to, stacked).astype(jnp.bfloat16), "lev", scatter_dimension=0, tiled=True
    ).astype(jnp.float32)
    nodes = fine_state.shape[1]
    old_state = both_modes[:, :nodes]
    old_tend = both_modes[:, nodes:]
    old_coarse = coarse_eval(old_state[:, 1:2])
    stiffness = (
        mode_decay[:, None, None, None]
        * (degree * (degree + 1.0) / (coarse * (coarse + 1.0)))[None, None]
    )
    source = old_tend - stiffness[:, None] * old_state
    integral_mid = (
        quad_weights[0][0] * source[:, 0]
        + quad_weights[0][1] * source[:, 1]
        + quad_weights[0][2] * source[:, 2]
    )
    integral_end = (
        quad_weights[1][0] * source[:, 0]
        + quad_weights[1][1] * source[:, 1]
        + quad_weights[1][2] * source[:, 2]
    )
    divisor = 1.0 + STEP_HALF * stiffness
    next_mid = (old_state[:, 0] + STEP_HALF * stiffness * old_state[:, 1] + integral_mid) / divisor
    coarse_fresh = coarse_eval(next_mid[:, None])
    next_end = (
        next_mid
        + STEP_HALF * (coarse_fresh[:, 0] - old_coarse[:, 0])
        + STEP_HALF * stiffness * old_state[:, 2]
        + integral_end
    ) / divisor
    change = jnp.stack([next_mid - old_state[:, 1], next_end - old_state[:, 2]], 1)
    lifted = lax.psum_scatter(
        mix(local_from, change).astype(jnp.bfloat16), "lev", scatter_dimension=0, tiled=True
    ).astype(jnp.float32)
    corrected = fine_state[:, 1:] + jnp.pad(
        lifted, ((0, 0), (0, 0), (0, 0), (0, 0), (0, fine_width + 1 - coarse))
    )
    return (corrected, fine_tend)


def solution(mesh):
    placed = (
        P("lev", None, None, "wave", None),
        P(),
        P("wave", "lev", None),
        P("lev"),
        P(),
        P(),
        P(),
        P(),
    )
    return jax.shard_map(
        per_device,
        mesh=mesh,
        in_specs=placed,
        out_specs=(P("lev", None, None, "wave", None), P("lev", None, None, "wave", None)),
        check_vma=False,
    )
```

profile of v0, /device:TPU:0, one launch (start us, length us, event | category | flops | bytes accessed | tf_op | source)
XLA Modules:
  0.0 130.4 jit_solution(1549815140402897033)
XLA Ops:
  0.7 0.7 broadcast_subtract_fusion.1
  1.5 6.2 %all_gather.9 = bf16[8,3,2,3,49]{4,2,3,1,0:T(2,128)(2,1)S(1)} all-gather(bf16[2,3,2,3,49]{4,2,3,1,0:T(2,128)(2,1)S(1)} %convert_element_type.212), channel_id=1, replica_groups=mesh['wave'=8,'lev'=4] {'lev'}, dimensions={0}, use_global_device_ids=true | all-gather | bytes 17640 | tf_op jit(solution)/shard_map/all_gather | solution.py:120
  7.7 0.7 copy-done.1
  8.7 0.8 reshape.468
  9.6 6.4 %all-to-all-start = ((bf16[8,2,432]{2,1,0:T(2,128)(2,1)}), bf16[8,2,432]{2,1,0:T(2,128)(2,1)S(1)}, u32[]{:S(2)}, u32[]{:S(2)}) async-start(bf16[8,2,432]{2,1,0:T(2,128)(2,1)} %reshape.468), calls=%async_computation | async-start | bytes 32768 | tf_op jit(solution)/shard_map/all_to_all | solution.py:122
  16.1 0.6 multiply_convert_fusion.3
  16.7 2.3 %multiply_convert_fusion.1 = (bf16[1,24,2,2560]{3,1,2,0:T(8,128)(2,1)S(1)}, bf16[1,24,2,2560]{3,1,2,0:T(8,128)(2,1)S(1)}) fusion(s32[24,2]{0,1:T(2,128)S(1)} %pad_add_fusion), kind=kLoop, calls=%fused_computation.52 | loop fusion | flops 1720320 | bytes 491712 | tf_op jit(solution)/shard_map/convert.4
  19.1 0.6 copy-done.6
  19.9 0.6 copy-done.7
  20.5 2.1 %all-to-all-done = bf16[8,2,432]{2,1,0:T(2,128)(2,1)S(1)} async-done(((bf16[8,2,432]{2,1,0:T(2,128)(2,1)}), bf16[8,2,432]{2,1,0:T(2,128)(2,1)S(1)}, u32[]{:S(2)}, u32[]{:S(2)}) %all-to-all-start) | async-done | bytes 13856 | tf_op jit(solution)/shard_map/all_to_all | solution.py:122
  22.6 0.2 reshape.469
  23.0 0.7 copy-done.3
  23.7 0.8 fusion.3
  24.7 0.8 reshape.470
  25.6 3.9 %all-to-all-start.1 = ((bf16[8,2,432]{2,1,0:T(2,128)(2,1)}), bf16[8,2,432]{2,1,0:T(2,128)(2,1)S(1)}, u32[]{:S(2)}, u32[]{:S(2)}) async-start(bf16[8,2,432]{2,1,0:T(2,128)(2,1)} %reshape.470), calls=%async_computation.1 | async-start | bytes 32768 | tf_op jit(solution)/shard_map/all_to_all | solution.py:123
  29.5 1.4 %slice.58 = f32[8,1280]{1,0:T(8,128)S(1)} slice(f32[8,2560]{1,0:T(8,128)S(1)} %copy-done.3), slice={[0:8:1], [0:2560:2]} | slice | bytes 81920 | tf_op jit(solution)/shard_map/slice | solution.py:85
  31.0 0.6 copy-done.8
  31.6 0.6 dynamic-slice
  32.9 3.2 %all-to-all-done.1 = bf16[8,2,432]{2,1,0:T(2,128)(2,1)S(1)} async-done(((bf16[8,2,432]{2,1,0:T(2,128)(2,1)}), bf16[8,2,432]{2,1,0:T(2,128)(2,1)S(1)}, u32[]{:S(2)}, u32[]{:S(2)}) %all-to-all-start.1) | async-done | bytes 13856 | tf_op jit(solution)/shard_map/all_to_all | solution.py:123
  36.0 0.2 reshape.471
  36.4 0.2 fusion
  36.7 10.5 %all-reduce.1 = bf16[8,3,2,3,49]{4,0,3,2,1:T(8,128)(2,1)S(1)} all-reduce(bf16[8,3,2,3,49]{4,0,3,2,1:T(8,128)(2,1)S(1)} %copy.103), channel_id=2, replica_groups=mesh['wave'=8,'lev'=4] {'lev'}, use_global_device_ids=true, to_apply=%region_1.2.clone | all-reduce | flops 7056 | bytes 28224
  47.2 0.3 convolution_convert_fusion
  47.6 11.7 %all-reduce.2 = bf16[8,6,2,3,24]{4,0,3,2,1:T(8,128)(2,1)S(1)} all-reduce(bf16[8,6,2,3,24]{4,0,3,2,1:T(8,128)(2,1)S(1)} %convolution_convert_fusion), channel_id=3, replica_groups=mesh['wave'=8,'lev'=4] {'lev'}, use_global_device_ids=true, to_apply=%region_2.3.clone | all-reduce | flops 6912 | bytes 27648
  59.4 5.2 %all_gather.10 = f32[8,1,2,3,24]{4,2,3,1,0:T(2,128)S(1)} all-gather(f32[2,1,2,3,24]{4,2,3,1,0:T(2,128)S(1)} %copy.104), channel_id=1, replica_groups=mesh['wave'=8,'lev'=4] {'lev'}, dimensions={0}, use_global_device_ids=true | all-gather | bytes 5760 | tf_op jit(solution)/shard_map/all_gather | solution.py:95
  64.9 0.7 copy.106
  65.6 3.3 %all-to-all-start.2 = ((bf16[8,1,2,3,1,24]{0,2,3,4,1,5:T(2,128)(2,1)}), bf16[8,1,2,3,1,24]{0,2,3,4,1,5:T(2,128)(2,1)S(1)}, u32[]{:S(2)}, u32[]{:S(2)}) async-start(bf16[8,1,2,3,1,24]{0,2,3,4,1,5:T(2,128)(2,1)} %copy.106), calls=%async_computation.2 | async-start | bytes 73728 | tf_op jit(solution)/shard_map/all_to_all | solution.py:111
  69.0 5.2 %all_gather.11 = f32[8,1,2,3,24]{4,2,3,1,0:T(2,128)S(1)} all-gather(f32[2,1,2,3,24]{4,2,3,1,0:T(2,128)S(1)} %copy.114), channel_id=1, replica_groups=mesh['wave'=8,'lev'=4] {'lev'}, dimensions={0}, use_global_device_ids=true | all-gather | bytes 5760 | tf_op jit(solution)/shard_map/all_gather | solution.py:95
  74.5 0.6 copy.125
  75.1 0.7 copy.116
  75.8 5.9 %all-to-all-start.4 = ((bf16[8,1,2,3,1,24]{0,2,3,4,1,5:T(2,128)(2,1)}), bf16[8,1,2,3,1,24]{0,2,3,4,1,5:T(2,128)(2,1)S(1)}, u32[]{:S(2)}, u32[]{:S(2)}) async-start(bf16[8,1,2,3,1,24]{0,2,3,4,1,5:T(2,128)(2,1)} %copy.116), calls=%async_computation.4 | async-start | bytes 73728 | tf_op jit(solution)/shard_map/all_to_all | solution.py:111
  81.8 0.4 fusion.21
  82.2 0.8 copy.110
  82.9 5.5 %all-to-all-done.4 = bf16[8,1,2,3,1,24]{0,2,3,4,1,5:T(2,128)(2,1)S(1)} async-done(((bf16[8,1,2,3,1,24]{0,2,3,4,1,5:T(2,128)(2,1)}), bf16[8,1,2,3,1,24]{0,2,3,4,1,5:T(2,128)(2,1)S(1)}, u32[]{:S(2)}, u32[]{:S(2)}) %all-to-all-start.4) | async-done | bytes 2336 | tf_op jit(solution)/shard_map/all_to_all | solution.py:111
  88.4 3.3 %all-to-all-start.3 = ((bf16[8,1,2,24,1,3]{0,2,5,4,1,3:T(2,128)(2,1)}), bf16[8,1,2,24,1,3]{0,2,5,4,1,3:T(2,128)(2,1)S(1)}, u32[]{:S(2)}, u32[]{:S(2)}) async-start(bf16[8,1,2,24,1,3]{0,2,5,4,1,3:T(2,128)(2,1)} %copy.110), calls=%async_computation.3 | async-start | bytes 73728 | tf_op jit(solution)/shard_map/all_to_all | solution.py:114
  91.9 0.4 fusion.18
  92.2 0.7 copy.120
  93.0 5.5 %all-to-all-done.3 = bf16[8,1,2,24,1,3]{0,2,5,4,1,3:T(2,128)(2,1)S(1)} async-done(((bf16[8,1,2,24,1,3]{0,2,5,4,1,3:T(2,128)(2,1)}), bf16[8,1,2,24,1,3]{0,2,5,4,1,3:T(2,128)(2,1)S(1)}, u32[]{:S(2)}, u32[]{:S(2)}) %all-to-all-start.3) | async-done | bytes 2336 | tf_op jit(solution)/shard_map/all_to_all | solution.py:114
  98.4 3.3 %all-to-all-start.5 = ((bf16[8,1,2,24,1,3]{0,2,5,4,1,3:T(2,128)(2,1)}), bf16[8,1,2,24,1,3]{0,2,5,4,1,3:T(2,128)(2,1)S(1)}, u32[]{:S(2)}, u32[]{:S(2)}) async-start(bf16[8,1,2,24,1,3]{0,2,5,4,1,3:T(2,128)(2,1)} %copy.120), calls=%async_computation.5 | async-start | bytes 73728 | tf_op jit(solution)/shard_map/all_to_all | solution.py:114
  101.8 0.2 fusion.7
  102.0 0.2 fusion.15
  102.2 6.2 %all-to-all-done.5 = bf16[8,1,2,24,1,3]{0,2,5,4,1,3:T(2,128)(2,1)S(1)} async-done(((bf16[8,1,2,24,1,3]{0,2,5,4,1,3:T(2,128)(2,1)}), bf16[8,1,2,24,1,3]{0,2,5,4,1,3:T(2,128)(2,1)S(1)}, u32[]{:S(2)}, u32[]{:S(2)}) %all-to-all-start.5) | async-done | bytes 2336 | tf_op jit(solution)/shard_map/all_to_all | solution.py:114
  108.5 0.2 fusion.9
  108.7 0.2 fusion.17
  108.8 10.3 %all-reduce.6 = (bf16[8,1,2,3,24]{4,0,3,2,1:T(8,128)(2,1)S(1)}, bf16[8,1,2,3,24]{4,0,3,2,1:T(8,128)(2,1)S(1)}) all-reduce(bf16[8,1,2,3,24]{4,0,3,2,1:T(8,128)(2,1)S(1)} %fusion.17, bf16[8,1,2,3,24]{4,0,3,2,1:T(8,128)(2,1)S(1)} %fusion.15), channel_id=5, replica_groups=mesh['wave'=8,'lev'=4] {'lev'}, use_global_device_ids=true, to_apply=%region_4.5.clone | all-reduce | flops 2304 | bytes 9216
  119.1 0.2 convolution_convert_fusion.2
  119.4 10.4 %all-reduce.5 = bf16[8,2,2,3,24]{4,0,3,2,1:T(8,128)(2,1)S(1)} all-reduce(bf16[8,2,2,3,24]{4,0,3,2,1:T(8,128)(2,1)S(1)} %convolution_convert_fusion.2), channel_id=6, replica_groups=mesh['wave'=8,'lev'=4] {'lev'}, use_global_device_ids=true, to_apply=%region_5.6.clone | all-reduce | flops 2304 | bytes 9216
  129.8 0.6 copy.124
  (53 shorter events, 2.2 us)
Async XLA Ops:
  0.6 46.6 %copy-start = (f32[8,8]{1,0:T(8,128)S(1)}, f32[8,8]{1,0:T(8,128)}, u32[]{:S(2)}) copy-start(f32[8,8]{1,0:T(8,128)} %param.14) | copy-start | bytes 772
  0.6 0.8 copy-start.2
  7.7 0.7 copy-start.1
  9.6 6.4 %copy-start.5 = (s32[24]{0:T(128)S(1)}, s32[24]{0:T(128)}, u32[]{:S(2)}) copy-start(s32[24]{0:T(128)} %param.9) | copy-start | bytes 292
  9.6 13.0 %all-to-all-start = ((bf16[8,2,432]{2,1,0:T(2,128)(2,1)}), bf16[8,2,432]{2,1,0:T(2,128)(2,1)S(1)}, u32[]{:S(2)}, u32[]{:S(2)}) async-start(bf16[8,2,432]{2,1,0:T(2,128)(2,1)} %reshape.468), calls=%async_computation | async-start | bytes 32768 | tf_op jit(solution)/shard_map/all_to_all | solution.py:122
  19.0 0.7 copy-start.6
  19.8 0.7 copy-start.7
  22.8 0.9 copy-start.3
  25.6 10.5 %all-to-all-start.1 = ((bf16[8,2,432]{2,1,0:T(2,128)(2,1)}), bf16[8,2,432]{2,1,0:T(2,128)(2,1)S(1)}, u32[]{:S(2)}, u32[]{:S(2)}) async-start(bf16[8,2,432]{2,1,0:T(2,128)(2,1)} %reshape.470), calls=%async_computation.1 | async-start | bytes 32768 | tf_op jit(solution)/shard_map/all_to_all | solution.py:123
  31.0 0.7 copy-start.8
  59.3 5.3 %copy-start.4 = (f32[8,8]{1,0:T(8,128)S(1)}, f32[8,8]{1,0:T(8,128)}, u32[]{:S(2)}) copy-start(f32[8,8]{1,0:T(8,128)} %param.13) | copy-start | bytes 772
  65.6 10.2 %all-to-all-start.2 = ((bf16[8,1,2,3,1,24]{0,2,3,4,1,5:T(2,128)(2,1)}), bf16[8,1,2,3,1,24]{0,2,3,4,1,5:T(2,128)(2,1)S(1)}, u32[]{:S(2)}, u32[]{:S(2)}) async-start(bf16[8,1,2,3,1,24]{0,2,3,4,1,5:T(2,128)(2,1)} %copy.106), calls=%async_computation.2 | async-start | bytes 73728 | tf_op jit(solution)/shard_map/all_to_all | solution.py:111
  75.8 12.6 %all-to-all-start.4 = ((bf16[8,1,2,3,1,24]{0,2,3,4,1,5:T(2,128)(2,1)}), bf16[8,1,2,3,1,24]{0,2,3,4,1,5:T(2,128)(2,1)S(1)}, u32[]{:S(2)}, u32[]{:S(2)}) async-start(bf16[8,1,2,3,1,24]{0,2,3,4,1,5:T(2,128)(2,1)} %copy.116), calls=%async_computation.4 | async-start | bytes 73728 | tf_op jit(solution)/shard_map/all_to_all | solution.py:111
  88.4 10.0 %all-to-all-start.3 = ((bf16[8,1,2,24,1,3]{0,2,5,4,1,3:T(2,128)(2,1)}), bf16[8,1,2,24,1,3]{0,2,5,4,1,3:T(2,128)(2,1)S(1)}, u32[]{:S(2)}, u32[]{:S(2)}) async-start(bf16[8,1,2,24,1,3]{0,2,5,4,1,3:T(2,128)(2,1)} %copy.110), calls=%async_computation.3 | async-start | bytes 73728 | tf_op jit(solution)/shard_map/all_to_all | solution.py:114
  98.4 10.0 %all-to-all-start.5 = ((bf16[8,1,2,24,1,3]{0,2,5,4,1,3:T(2,128)(2,1)}), bf16[8,1,2,24,1,3]{0,2,5,4,1,3:T(2,128)(2,1)S(1)}, u32[]{:S(2)}, u32[]{:S(2)}) async-start(bf16[8,1,2,24,1,3]{0,2,5,4,1,3:T(2,128)(2,1)} %copy.120), calls=%async_computation.5 | async-start | bytes 73728 | tf_op jit(solution)/shard_map/all_to_all | solution.py:114
where the time goes:
time: 131 us; the launch traced here: 130 us
  blocking collectives  59.5 us (45%)
  starting transfers between devices  26.3 us (20%)
  waiting for transfers between devices  22.5 us (17%)
  local copies, waits for them, and re-layouts  12.5 us (10%)
  other arithmetic  4.17 us (3%)
  matrix products  3.8 us (3%)
  between operations  1.69 us (1%)
    unnamed x4, blocking collectives  42.8 us
    all_to_all x2, waiting for transfers between devices, coarse_eval(): lax.all_to_all(coarse_grid_step(fourier), 'wave', split_axis=3, concat_ax...  11.7 us
    all_gather x2, blocking collectives, coarse_start(): gathered = lax.all_gather(modes, 'lev', axis=0, tiled=True)  10.4 us
    all_to_all x2, starting transfers between devices, coarse_eval(): lax.all_to_all(coarse_start(modes), 'wave', split_axis=5, concat_axis=3,...  9.25 us
    unnamed x26, local copies, waits for them, and re-layouts  7.27 us
    all_to_all x2, starting transfers between devices, coarse_eval(): lax.all_to_all(coarse_grid_step(fourier), 'wave', split_axis=3, concat_ax...  6.68 us
    all_to_all x1, starting transfers between devices, per_device(): lax.all_to_all(fine_fourier, 'wave', split_axis=5, concat_axis=3, tiled=T...  6.43 us
    all_gather x1, blocking collectives, per_device(): lax.all_gather(fine_state.astype(jnp.bfloat16), 'lev', axis=0, tiled=True)  6.21 us
  transfers between devices with their start and end apart: 6, of which 5 were waited for; matrix products, arithmetic and copies ran while one was open for 7% of the time, Pallas kernels for 0%

commit v1 on v0

--- a/solution.py
+++ b/solution.py
@@ -92,7 +92,9 @@
         return mix(modes_to, partial_sum)
 
     def coarse_start(modes):
-        gathered = lax.all_gather(modes, "lev", axis=0, tiled=True)
+        gathered = jnp.concatenate(
+            lax.all_to_all(jnp.stack([modes] * lax.axis_size("lev")), "lev", 0, 0), axis=0
+        )
         levels = (mix(modes_from, gathered) * keep_float).astype(jnp.bfloat16)
         return legendre_inverse(levels, coarse_leg, keep_mask)
 

time: 131 us -> 137 us (1.046)
  blocking collectives: 59.5 us -> 49.3 us
  waiting for transfers between devices: 22.5 us -> 30.5 us
  starting transfers between devices: 26.3 us -> 30.1 us
  local copies, waits for them, and re-layouts: 12.5 us -> 15.3 us
    all_gather x2 -> x0, blocking collectives: 10.4 us -> none  [coarse_start(): gathered = lax.all_gather(modes, 'lev', axis=0, tiled=True)]
    all_to_all x0 -> x2, starting transfers between devices: none -> 6.45 us  [coarse_start(): lax.all_to_all(jnp.stack([modes] * lax.axis_size('lev')), 'lev', 0, 0)]
    all_to_all x2, waiting for transfers between devices: 5.53 us -> 10.3 us  [coarse_eval(): lax.all_to_all(coarse_start(modes), 'wave', split_axis=5, concat_axis=3,...]
    all_to_all x0 -> x2, waiting for transfers between devices: none -> 3.19 us  [coarse_start(): lax.all_to_all(jnp.stack([modes] * lax.axis_size('lev')), 'lev', 0, 0)]
    all_to_all x2, starting transfers between devices: 9.25 us -> 6.68 us  [coarse_eval(): lax.all_to_all(coarse_start(modes), 'wave', split_axis=5, concat_axis=3,...]
    unnamed x26 -> x32, local copies, waits for them, and re-layouts: 7.27 us -> 9.5 us
  transfers between devices with their start and end apart: 6 -> 8, of which waited for: 5 -> 8; matrix products, arithmetic and copies ran while one was open for 7% -> 10% of each run, Pallas kernels for 0% -> 0%
where the time goes in v1:
time: 137 us; the launch traced here: 136 us
  blocking collectives  49.3 us (36%)
  waiting for transfers between devices  30.5 us (22%)
  starting transfers between devices  30.1 us (22%)
  local copies, waits for them, and re-layouts  15.3 us (11%)
  other arithmetic  5.48 us (4%)
  matrix products  3.8 us (3%)
  between operations  1.77 us (1%)
    unnamed x4, blocking collectives  43.1 us
    all_to_all x2, waiting for transfers between devices, coarse_eval(): lax.all_to_all(coarse_grid_step(fourier), 'wave', split_axis=3, concat_ax...  11.7 us
    all_to_all x2, waiting for transfers between devices, coarse_eval(): lax.all_to_all(coarse_start(modes), 'wave', split_axis=5, concat_axis=3,...  10.3 us
    unnamed x32, local copies, waits for them, and re-layouts  9.5 us
    all_to_all x2, starting transfers between devices, coarse_eval(): lax.all_to_all(coarse_start(modes), 'wave', split_axis=5, concat_axis=3,...  6.68 us
    all_to_all x2, starting transfers between devices, coarse_eval(): lax.all_to_all(coarse_grid_step(fourier), 'wave', split_axis=3, concat_ax...  6.68 us
    all_to_all x2, starting transfers between devices, coarse_start(): lax.all_to_all(jnp.stack([modes] * lax.axis_size('lev')), 'lev', 0, 0)  6.45 us
    all_to_all x1, starting transfers between devices, per_device(): lax.all_to_all(fine_fourier, 'wave', split_axis=5, concat_axis=3, tiled=T...  6.43 us
  transfers between devices with their start and end apart: 8, of which 8 were waited for; matrix products, arithmetic and copies ran while one was open for 10% of the time, Pallas kernels for 0%

profile of v1, /device:TPU:0, one launch (start us, length us, event | category | flops | bytes accessed | tf_op | source)
XLA Modules:
  0.0 136.3 jit_solution(5797076958305102702)
XLA Ops:
  0.7 0.7 broadcast_subtract_fusion.1
  1.5 6.2 %all_gather.3 = bf16[8,3,2,3,49]{4,2,3,1,0:T(2,128)(2,1)S(1)} all-gather(bf16[2,3,2,3,49]{4,2,3,1,0:T(2,128)(2,1)S(1)} %convert_element_type.212), channel_id=1, replica_groups=mesh['wave'=8,'lev'=4] {'lev'}, dimensions={0}, use_global_device_ids=true | all-gather | bytes 17640 | tf_op jit(solution)/shard_map/all_gather | solution.py:122
  7.7 0.7 copy-done.1
  8.7 0.8 reshape.482
  9.6 6.4 %all-to-all-start = ((bf16[8,2,432]{2,1,0:T(2,128)(2,1)}), bf16[8,2,432]{2,1,0:T(2,128)(2,1)S(1)}, u32[]{:S(2)}, u32[]{:S(2)}) async-start(bf16[8,2,432]{2,1,0:T(2,128)(2,1)} %reshape.482), calls=%async_computation | async-start | bytes 32768 | tf_op jit(solution)/shard_map/all_to_all | solution.py:124
  16.1 0.6 multiply_convert_fusion.3
  16.7 2.3 %multiply_convert_fusion.1 = (bf16[1,24,2,2560]{3,1,2,0:T(8,128)(2,1)S(1)}, bf16[1,24,2,2560]{3,1,2,0:T(8,128)(2,1)S(1)}) fusion(s32[24,2]{0,1:T(2,128)S(1)} %pad_add_fusion), kind=kLoop, calls=%fused_computation.52 | loop fusion | flops 1720320 | bytes 491712 | tf_op jit(solution)/shard_map/convert.4
  19.1 0.6 copy-done.6
  19.9 0.6 copy-done.7
  20.5 2.1 %all-to-all-done = bf16[8,2,432]{2,1,0:T(2,128)(2,1)S(1)} async-done(((bf16[8,2,432]{2,1,0:T(2,128)(2,1)}), bf16[8,2,432]{2,1,0:T(2,128)(2,1)S(1)}, u32[]{:S(2)}, u32[]{:S(2)}) %all-to-all-start) | async-done | bytes 13856 | tf_op jit(solution)/shard_map/all_to_all | solution.py:124
  23.0 0.7 copy-done.3
  23.7 0.8 fusion.3
  24.7 0.8 reshape.484
  25.6 3.9 %all-to-all-start.1 = ((bf16[8,2,432]{2,1,0:T(2,128)(2,1)}), bf16[8,2,432]{2,1,0:T(2,128)(2,1)S(1)}, u32[]{:S(2)}, u32[]{:S(2)}) async-start(bf16[8,2,432]{2,1,0:T(2,128)(2,1)} %reshape.484), calls=%async_computation.1 | async-start | bytes 32768 | tf_op jit(solution)/shard_map/all_to_all | solution.py:125
  29.5 1.4 %slice.60 = f32[8,1280]{1,0:T(8,128)S(1)} slice(f32[8,2560]{1,0:T(8,128)S(1)} %copy-done.3), slice={[0:8:1], [0:2560:2]} | slice | bytes 81920 | tf_op jit(solution)/shard_map/slice | solution.py:85
  31.0 0.6 copy-done.8
  31.6 0.6 dynamic-slice
  32.9 3.2 %all-to-all-done.1 = bf16[8,2,432]{2,1,0:T(2,128)(2,1)S(1)} async-done(((bf16[8,2,432]{2,1,0:T(2,128)(2,1)}), bf16[8,2,432]{2,1,0:T(2,128)(2,1)S(1)}, u32[]{:S(2)}, u32[]{:S(2)}) %all-to-all-start.1) | async-done | bytes 13856 | tf_op jit(solution)/shard_map/all_to_all | solution.py:125
  36.7 10.5 %all-reduce.1 = bf16[8,3,2,3,49]{4,0,3,2,1:T(8,128)(2,1)S(1)} all-reduce(bf16[8,3,2,3,49]{4,0,3,2,1:T(8,128)(2,1)S(1)} %copy.107), channel_id=2, replica_groups=mesh['wave'=8,'lev'=4] {'lev'}, use_global_device_ids=true, to_apply=%region_1.2.clone | all-reduce | flops 7056 | bytes 28224
  47.6 11.7 %all-reduce.2 = bf16[8,6,2,3,24]{4,0,3,2,1:T(8,128)(2,1)S(1)} all-reduce(bf16[8,6,2,3,24]{4,0,3,2,1:T(8,128)(2,1)S(1)} %convolution_convert_fusion), channel_id=3, replica_groups=mesh['wave'=8,'lev'=4] {'lev'}, use_global_device_ids=true, to_apply=%region_2.3.clone | all-reduce | flops 6912 | bytes 27648
  59.4 0.7 reshape.488
  60.1 3.2 %all-to-all-start.2 = ((f32[4,1,288]{2,1,0:T(1,128)}), f32[4,1,288]{2,1,0:T(1,128)S(1)}, u32[]{:S(2)}, u32[]{:S(2)}) async-start(f32[4,1,288]{2,1,0:T(1,128)} %reshape.488), calls=%async_computation.2 | async-start | bytes 12288 | tf_op jit(solution)/shard_map/all_to_all | solution.py:96
  63.3 0.6 copy.129
  63.9 0.7 reshape.486
  64.6 2.4 %all-to-all-done.2 = f32[4,1,288]{2,1,0:T(1,128)S(1)} async-done(((f32[4,1,288]{2,1,0:T(1,128)}), f32[4,1,288]{2,1,0:T(1,128)S(1)}, u32[]{:S(2)}, u32[]{:S(2)}) %all-to-all-start.2) | async-done | bytes 4640 | tf_op jit(solution)/shard_map/all_to_all | solution.py:96
  67.1 3.2 %all-to-all-start.5 = ((f32[4,1,288]{2,1,0:T(1,128)}), f32[4,1,288]{2,1,0:T(1,128)S(1)}, u32[]{:S(2)}, u32[]{:S(2)}) async-start(f32[4,1,288]{2,1,0:T(1,128)} %reshape.486), calls=%async_computation.5 | async-start | bytes 12288 | tf_op jit(solution)/shard_map/all_to_all | solution.py:96
  70.3 0.5 broadcast.461
  70.9 0.7 reduce.2
  71.7 0.7 copy-done.4
  72.6 0.7 copy.110
  73.3 0.8 all-to-all-done.5
  74.1 3.3 %all-to-all-start.3 = ((bf16[8,1,2,3,1,24]{0,2,3,4,1,5:T(2,128)(2,1)}), bf16[8,1,2,3,1,24]{0,2,3,4,1,5:T(2,128)(2,1)S(1)}, u32[]{:S(2)}, u32[]{:S(2)}) async-start(bf16[8,1,2,3,1,24]{0,2,3,4,1,5:T(2,128)(2,1)} %copy.110), calls=%async_computation.3 | async-start | bytes 73728 | tf_op jit(solution)/shard_map/all_to_all | solution.py:113
  77.4 0.7 reduce.1
  78.5 0.7 copy.120
  79.2 4.9 %all-to-all-done.3 = bf16[8,1,2,3,1,24]{0,2,3,4,1,5:T(2,128)(2,1)S(1)} async-done(((bf16[8,1,2,3,1,24]{0,2,3,4,1,5:T(2,128)(2,1)}), bf16[8,1,2,3,1,24]{0,2,3,4,1,5:T(2,128)(2,1)S(1)}, u32[]{:S(2)}, u32[]{:S(2)}) %all-to-all-start.3) | async-done | bytes 2336 | tf_op jit(solution)/shard_map/all_to_all | solution.py:113
  84.1 3.3 %all-to-all-start.6 = ((bf16[8,1,2,3,1,24]{0,2,3,4,1,5:T(2,128)(2,1)}), bf16[8,1,2,3,1,24]{0,2,3,4,1,5:T(2,128)(2,1)S(1)}, u32[]{:S(2)}, u32[]{:S(2)}) async-start(bf16[8,1,2,3,1,24]{0,2,3,4,1,5:T(2,128)(2,1)} %copy.120), calls=%async_computation.6 | async-start | bytes 73728 | tf_op jit(solution)/shard_map/all_to_all | solution.py:113
  87.5 0.4 fusion.21
  87.9 0.8 copy.114
  88.6 5.5 %all-to-all-done.6 = bf16[8,1,2,3,1,24]{0,2,3,4,1,5:T(2,128)(2,1)S(1)} async-done(((bf16[8,1,2,3,1,24]{0,2,3,4,1,5:T(2,128)(2,1)}), bf16[8,1,2,3,1,24]{0,2,3,4,1,5:T(2,128)(2,1)S(1)}, u32[]{:S(2)}, u32[]{:S(2)}) %all-to-all-start.6) | async-done | bytes 2336 | tf_op jit(solution)/shard_map/all_to_all | solution.py:113
  94.1 3.3 %all-to-all-start.4 = ((bf16[8,1,2,24,1,3]{0,2,5,4,1,3:T(2,128)(2,1)}), bf16[8,1,2,24,1,3]{0,2,5,4,1,3:T(2,128)(2,1)S(1)}, u32[]{:S(2)}, u32[]{:S(2)}) async-start(bf16[8,1,2,24,1,3]{0,2,5,4,1,3:T(2,128)(2,1)} %copy.114), calls=%async_computation.4 | async-start | bytes 73728 | tf_op jit(solution)/shard_map/all_to_all | solution.py:116
  97.5 0.4 fusion.18
  97.9 0.8 copy.124
  98.6 5.5 %all-to-all-done.4 = bf16[8,1,2,24,1,3]{0,2,5,4,1,3:T(2,128)(2,1)S(1)} async-done(((bf16[8,1,2,24,1,3]{0,2,5,4,1,3:T(2,128)(2,1)}), bf16[8,1,2,24,1,3]{0,2,5,4,1,3:T(2,128)(2,1)S(1)}, u32[]{:S(2)}, u32[]{:S(2)}) %all-to-all-start.4) | async-done | bytes 2336 | tf_op jit(solution)/shard_map/all_to_all | solution.py:116
  104.1 3.3 %all-to-all-start.7 = ((bf16[8,1,2,24,1,3]{0,2,5,4,1,3:T(2,128)(2,1)}), bf16[8,1,2,24,1,3]{0,2,5,4,1,3:T(2,128)(2,1)S(1)}, u32[]{:S(2)}, u32[]{:S(2)}) async-start(bf16[8,1,2,24,1,3]{0,2,5,4,1,3:T(2,128)(2,1)} %copy.124), calls=%async_computation.7 | async-start | bytes 73728 | tf_op jit(solution)/shard_map/all_to_all | solution.py:116
  107.8 6.2 %all-to-all-done.7 = bf16[8,1,2,24,1,3]{0,2,5,4,1,3:T(2,128)(2,1)S(1)} async-done(((bf16[8,1,2,24,1,3]{0,2,5,4,1,3:T(2,128)(2,1)}), bf16[8,1,2,24,1,3]{0,2,5,4,1,3:T(2,128)(2,1)S(1)}, u32[]{:S(2)}, u32[]{:S(2)}) %all-to-all-start.7) | async-done | bytes 2336 | tf_op jit(solution)/shard_map/all_to_all | solution.py:116
  114.5 10.3 %all-reduce.6 = (bf16[8,1,2,3,24]{4,0,3,2,1:T(8,128)(2,1)S(1)}, bf16[8,1,2,3,24]{4,0,3,2,1:T(8,128)(2,1)S(1)}) all-reduce(bf16[8,1,2,3,24]{4,0,3,2,1:T(8,128)(2,1)S(1)} %fusion.17, bf16[8,1,2,3,24]{4,0,3,2,1:T(8,128)(2,1)S(1)} %fusion.15), channel_id=5, replica_groups=mesh['wave'=8,'lev'=4] {'lev'}, use_global_device_ids=true, to_apply=%region_4.5.clone | all-reduce | flops 2304 | bytes 9216
  125.0 10.6 %all-reduce.5 = bf16[8,2,2,3,24]{4,0,3,2,1:T(8,128)(2,1)S(1)} all-reduce(bf16[8,2,2,3,24]{4,0,3,2,1:T(8,128)(2,1)S(1)} %convolution_convert_fusion.2), channel_id=6, replica_groups=mesh['wave'=8,'lev'=4] {'lev'}, use_global_device_ids=true, to_apply=%region_5.6.clone | all-reduce | flops 2304 | bytes 9216
  135.7 0.6 copy.128
  (66 shorter events, 4.4 us)
Async XLA Ops:
  0.6 46.6 %copy-start = (f32[8,8]{1,0:T(8,128)S(1)}, f32[8,8]{1,0:T(8,128)}, u32[]{:S(2)}) copy-start(f32[8,8]{1,0:T(8,128)} %param.14) | copy-start | bytes 772
  0.6 0.8 copy-start.2
  7.7 0.7 copy-start.1
  9.6 6.4 %copy-start.5 = (s32[24]{0:T(128)S(1)}, s32[24]{0:T(128)}, u32[]{:S(2)}) copy-start(s32[24]{0:T(128)} %param.9) | copy-start | bytes 292
  9.6 13.0 %all-to-all-start = ((bf16[8,2,432]{2,1,0:T(2,128)(2,1)}), bf16[8,2,432]{2,1,0:T(2,128)(2,1)S(1)}, u32[]{:S(2)}, u32[]{:S(2)}) async-start(bf16[8,2,432]{2,1,0:T(2,128)(2,1)} %reshape.482), calls=%async_computation | async-start | bytes 32768 | tf_op jit(solution)/shard_map/all_to_all | solution.py:124
  19.0 0.7 copy-start.6
  19.8 0.7 copy-start.7
  22.8 0.9 copy-start.3
  25.6 10.5 %all-to-all-start.1 = ((bf16[8,2,432]{2,1,0:T(2,128)(2,1)}), bf16[8,2,432]{2,1,0:T(2,128)(2,1)S(1)}, u32[]{:S(2)}, u32[]{:S(2)}) async-start(bf16[8,2,432]{2,1,0:T(2,128)(2,1)} %reshape.484), calls=%async_computation.1 | async-start | bytes 32768 | tf_op jit(solution)/shard_map/all_to_all | solution.py:125
  31.0 0.7 copy-start.8
  60.1 7.0 %all-to-all-start.2 = ((f32[4,1,288]{2,1,0:T(1,128)}), f32[4,1,288]{2,1,0:T(1,128)S(1)}, u32[]{:S(2)}, u32[]{:S(2)}) async-start(f32[4,1,288]{2,1,0:T(1,128)} %reshape.488), calls=%async_computation.2 | async-start | bytes 12288 | tf_op jit(solution)/shard_map/all_to_all | solution.py:96
  67.1 7.0 %all-to-all-start.5 = ((f32[4,1,288]{2,1,0:T(1,128)}), f32[4,1,288]{2,1,0:T(1,128)S(1)}, u32[]{:S(2)}, u32[]{:S(2)}) async-start(f32[4,1,288]{2,1,0:T(1,128)} %reshape.486), calls=%async_computation.5 | async-start | bytes 12288 | tf_op jit(solution)/shard_map/all_to_all | solution.py:96
  71.6 0.7 copy-start.4
  74.1 10.0 %all-to-all-start.3 = ((bf16[8,1,2,3,1,24]{0,2,3,4,1,5:T(2,128)(2,1)}), bf16[8,1,2,3,1,24]{0,2,3,4,1,5:T(2,128)(2,1)S(1)}, u32[]{:S(2)}, u32[]{:S(2)}) async-start(bf16[8,1,2,3,1,24]{0,2,3,4,1,5:T(2,128)(2,1)} %copy.110), calls=%async_computation.3 | async-start | bytes 73728 | tf_op jit(solution)/shard_map/all_to_all | solution.py:113
  84.1 10.0 %all-to-all-start.6 = ((bf16[8,1,2,3,1,24]{0,2,3,4,1,5:T(2,128)(2,1)}), bf16[8,1,2,3,1,24]{0,2,3,4,1,5:T(2,128)(2,1)S(1)}, u32[]{:S(2)}, u32[]{:S(2)}) async-start(bf16[8,1,2,3,1,24]{0,2,3,4,1,5:T(2,128)(2,1)} %copy.120), calls=%async_computation.6 | async-start | bytes 73728 | tf_op jit(solution)/shard_map/all_to_all | solution.py:113
  94.1 10.0 %all-to-all-start.4 = ((bf16[8,1,2,24,1,3]{0,2,5,4,1,3:T(2,128)(2,1)}), bf16[8,1,2,24,1,3]{0,2,5,4,1,3:T(2,128)(2,1)S(1)}, u32[]{:S(2)}, u32[]{:S(2)}) async-start(bf16[8,1,2,24,1,3]{0,2,5,4,1,3:T(2,128)(2,1)} %copy.114), calls=%async_computation.4 | async-start | bytes 73728 | tf_op jit(solution)/shard_map/all_to_all | solution.py:116
  104.1 10.0 %all-to-all-start.7 = ((bf16[8,1,2,24,1,3]{0,2,5,4,1,3:T(2,128)(2,1)}), bf16[8,1,2,24,1,3]{0,2,5,4,1,3:T(2,128)(2,1)S(1)}, u32[]{:S(2)}, u32[]{:S(2)}) async-start(bf16[8,1,2,24,1,3]{0,2,5,4,1,3:T(2,128)(2,1)} %copy.124), calls=%async_computation.7 | async-start | bytes 73728 | tf_op jit(solution)/shard_map/all_to_all | solution.py:116
